TPU v7x, 512 devices: a whole 4x4x16 slice. The times are simulated.
512 devices in a mesh: section: 4 (over y_hi, core), fsdp: 32 (over y_lo, z), ep: 4 (over x).
Axes of the slice: x: 4, y: 4 (y_hi: 2, y_lo: 2; y = y_hi * 2 + y_lo), z: 16, core: 2. Of those that a mesh axis runs over, the one named last changes fastest.
Arguments:
- hidden: bfloat16 [32768, 7168], P(('section', 'fsdp'), 'ep'), may hold values from -6 to 6
- attn_gain: float32 [7168], replicated, may hold values from 0.25 to 1.75
- q_gain: float32 [1536], replicated, may hold values from 0.25 to 1.75
- kv_gain: float32 [512], replicated, may hold values from 0.25 to 1.75
- down_weight: bfloat16 [7168, 2112], P('fsdp', 'ep'), may hold values from -0.0625 to 0.0625
Outputs:
- q_latent: bfloat16 [32768, 1536], P(('section', 'fsdp', 'ep'))
- kv_cache: bfloat16 [32768, 576], P(('section', 'fsdp', 'ep'))
All inputs are finite; a program needn't handle non-finite values.
Results may differ from a plain program's by a relative error of at most 0.0049.
Values may be sent and summed in bfloat16 or wider, within the bound.
A program may use at most 64 MiB of HBM per device.

v0:
```python
import jax
import jax.numpy as jnp
from jax import lax
from jax.sharding import PartitionSpec as P

QL = 1536
KVL = 512
ROPE = 64
LENGTH = 4096
epsilon = 1e-06
rope_base = 10000.0


def from_behind(x, axis, by):
    count = lax.axis_size(axis)
    return lax.ppermute(x, axis, [(i, (i + by) % count) for i in range(count)])


def root_scale(values, gain):
    mean_square = jnp.mean(values * values, axis=-1, keepdims=True)
    return values * lax.rsqrt(mean_square + epsilon) * gain


def rotate(latent, position):
    half_rope = ROPE // 2
    frequency = rope_base ** (-(jnp.arange(half_rope).astype(jnp.float32) / half_rope))
    angle = position.astype(jnp.float32)[:, None] * frequency[None, :]
    first = latent[:, QL + KVL : QL + KVL + half_rope]
    second = latent[:, QL + KVL + half_rope :]
    cosine = jnp.cos(angle)
    sine = jnp.sin(angle)
    return jnp.concatenate([first * cosine - second * sine, second * cosine + first * sine], axis=1)


def on_device(hidden, attn_gain, q_gain, kv_gain, down_weight):
    row_count = hidden.shape[0]
    moved = from_behind(hidden, "section", 1)
    whole = lax.all_gather(moved, "ep", axis=1, tiled=True)
    normed = root_scale(whole.astype(jnp.float32), attn_gain).astype(jnp.bfloat16)
    partial_latent = jnp.dot(
        normed,
        lax.all_gather(down_weight, "fsdp", axis=0, tiled=True),
        preferred_element_type=jnp.float32,
    )
    latent = lax.all_to_all(partial_latent, "ep", split_axis=0, concat_axis=1, tiled=True)
    quarter = latent.shape[0]
    query = root_scale(latent[:, :QL], q_gain).astype(jnp.bfloat16)
    key_value = root_scale(latent[:, QL : QL + KVL], kv_gain)
    row_index = (
        lax.axis_index("fsdp") * row_count + lax.axis_index("ep") * quarter + jnp.arange(quarter)
    )
    position = row_index % LENGTH
    cache = jnp.concatenate([key_value, rotate(latent, position)], axis=1).astype(jnp.bfloat16)
    return (query, cache)


def solution(mesh):
    placed = (P(("section", "fsdp"), "ep"), P(), P(), P(), P("fsdp", "ep"))
    return jax.shard_map(
        on_device,
        mesh=mesh,
        in_specs=placed,
        out_specs=(P(("section", "fsdp", "ep"), None), P(("section", "fsdp", "ep"), None)),
        check_vma=False,
    )
```

profile of v0, /device:TPU:16, one launch (start us, length us, event | category | flops | bytes accessed | tf_op | source)
XLA Modules:
  0.0 287.9 jit_solution(6684082173452654898)
XLA Ops:
  7.2 0.0 all-gather.4.cloned.1.call-start
  7.2 1.9 collective-permute-start
  9.1 14.5 %collective-permute-done = bf16[256,1792]{1,0:T(8,128)(2,1)S(1)} collective-permute-done((bf16[256,1792]{1,0:T(8,128)(2,1)}, bf16[256,1792]{1,0:T(8,128)(2,1)S(1)}, u32[]{:S(2)}, u32[]{:S(2)}) %collective-permute-start) | collective-permute-done | bytes 917536 | tf_op jit(solution)/shard_map/ppermute | solution.py:16
  23.6 0.0 copy-start
  23.6 1.0 copy-done
  24.7 0.0 all-gather.4.cloned.1.call-update
  24.7 0.0 all-gather.6.cloned.1.call-start
  24.7 0.7 all-gather.6.cloned.1.call-update
  25.4 55.2 %all-gather.4.cloned.1.call-done = bf16[256,7168]{1,0:T(8,128)(2,1)} async-done(((bf16[256,1792]{1,0:T(8,128)(2,1)}), bf16[256,7168]{1,0:T(8,128)(2,1)}) %all-gather.4.cloned.1.call-update) | async-done | bytes 3670032 | tf_op jit(solution)/shard_map/all_gather | solution.py:38
  80.6 2.8 fusion
  83.5 147.0 %all-gather.6.cloned.1.call-done = bf16[32,224,528]{1,2,0:T(8,128)(2,1)} async-done(((bf16[1,224,528]{1,2,0:T(8,128)(2,1)}), bf16[32,224,528]{1,2,0:T(8,128)(2,1)}) %all-gather.6.cloned.1.call-update) | async-done | bytes 7569424 | tf_op jit(solution)/shard_map/all_gather | solution.py:42
  230.5 9.9 %copy.16 = bf16[32,224,528]{1,0,2:T(8,128)(2,1)} copy(bf16[32,224,528]{1,2,0:T(8,128)(2,1)} %all-gather.6.cloned.1.call-done) | data formatting | bytes 15138816 | tf_op jit(solution)/shard_map/all_gather | solution.py:42
  240.4 16.7 %reshape.58 = bf16[7168,528]{0,1:T(8,128)(2,1)} reshape(bf16[32,224,528]{1,0,2:T(8,128)(2,1)} %copy.16) | data formatting | bytes 15138816
  257.0 0.0 copy-done.3
  257.0 8.2 %fusion.3 = f32[256,528]{1,0:T(8,128)} fusion(bf16[7168,528]{0,1:T(8,128)(2,1)} %reshape.58, bf16[256,7168]{1,0:T(8,128)(2,1)} %all-gather.4.cloned.1.call-done, f32[7168]{0:T(1024)S(1)} %copy-done.3, f32[256]{0:T(256)S(1)} %add_rsqrt_fusion), kind=kOutput, calls=%fused_computation.5 | convolution fusion | flops 1945108480 | bytes 11809792 | tf_op jit(solution)/shard_map/dot_general | solution.py:40
  265.3 3.8 %all-to-all-start = ((f32[4,64,528]{2,1,0:T(8,128)}), f32[4,64,528]{2,1,0:T(8,128)S(1)}, u32[]{:S(2)}, u32[]{:S(2)}) async-start(f32[4,64,528]{2,1,0:T(8,128)} %bitcast.1), calls=%async_computation | async-start | bytes 1310720 | tf_op jit(solution)/shard_map/all_to_all | solution.py:45
  269.1 8.8 %all-to-all-done = f32[4,64,528]{2,1,0:T(8,128)S(1)} async-done(((f32[4,64,528]{2,1,0:T(8,128)}), f32[4,64,528]{2,1,0:T(8,128)S(1)}, u32[]{:S(2)}, u32[]{:S(2)}) %all-to-all-start) | async-done | bytes 540704 | tf_op jit(solution)/shard_map/all_to_all | solution.py:45
  277.8 0.4 copy.18
  278.3 0.3 all_to_all.17
  278.6 0.1 multiply_reduce_fusion
  278.7 0.1 fusion.17
  278.8 0.1 multiply_reduce_fusion.1
  278.9 0.1 copy.25
  279.0 0.1 copy.24
  279.1 0.2 fusion.12
  279.2 0.1 copy.22
  279.3 0.1 copy.21
  279.5 0.0 copy-done.1
  279.5 0.8 multiply_convert_fusion
  280.3 0.0 copy-done.2
  280.3 0.1 multiply_convert_fusion.1
  280.3 0.7 pad_maximum_fusion
  (8 shorter events, 0.0 us)
Async XLA Ops:
  7.2 73.5 %all-gather.4.cloned.1.call-start = ((), (), s32[]{:S(2)}) async-start(), calls=%async_computation.1 | async-start | bytes 4587520 | tf_op jit(solution)/shard_map/all_gather | solution.py:38
  7.2 16.4 %collective-permute-start = (bf16[256,1792]{1,0:T(8,128)(2,1)}, bf16[256,1792]{1,0:T(8,128)(2,1)S(1)}, u32[]{:S(2)}, u32[]{:S(2)}) collective-permute-start(bf16[256,1792]{1,0:T(8,128)(2,1)} %param.5), channel_id=1, source_target_pairs={{0,128},{128,256},{256,384},{384,0},{1,129},{129,257},{257,385},{3... | collective-permute-start | bytes 2752520 | tf_op jit(solution)/shard_map/ppermute | solution.py:16
  23.6 1.0 copy-start
  24.7 205.8 %all-gather.6.cloned.1.call-start = ((), (), s32[]{:S(2)}) async-start(), calls=%async_computation.2 | async-start | bytes 8921088 | tf_op jit(solution)/shard_map/all_gather | solution.py:42
  240.4 16.7 %copy-start.3 = (f32[7168]{0:T(1024)S(1)}, f32[7168]{0:T(1024)}, u32[]{:S(2)}) copy-start(f32[7168]{0:T(1024)} %param.6) | copy-start | bytes 86020
  257.0 22.4 %copy-start.1 = (f32[1536]{0:T(1024)S(1)}, f32[1536]{0:T(1024)}, u32[]{:S(2)}) copy-start(f32[1536]{0:T(1024)} %param.7) | copy-start | bytes 18436
  257.0 23.2 %copy-start.2 = (f32[512]{0:T(512)S(1)}, f32[512]{0:T(512)}, u32[]{:S(2)}) copy-start(f32[512]{0:T(512)} %param.8) | copy-start | bytes 6148
  265.3 12.6 %all-to-all-start = ((f32[4,64,528]{2,1,0:T(8,128)}), f32[4,64,528]{2,1,0:T(8,128)S(1)}, u32[]{:S(2)}, u32[]{:S(2)}) async-start(f32[4,64,528]{2,1,0:T(8,128)} %bitcast.1), calls=%async_computation | async-start | bytes 1310720 | tf_op jit(solution)/shard_map/all_to_all | solution.py:45
Sparse Core Ops, SparseCore 0:
  24.8 55.7 all-gather.3
  82.7 147.7 all-gather.5
where the time goes:
time: 289 us; the launch traced here: 288 us
  waiting for transfers between devices  226 us (78%)
  local copies, waits for them, and re-layouts  28.7 us (10%)
  between operations  14.1 us (5%)
  matrix products  8.22 us (3%)
  starting transfers between devices  5.8 us (2%)
  other arithmetic  4.86 us (2%)
    all_gather x1, waiting for transfers between devices, on_device(): lax.all_gather(down_weight, 'fsdp', axis=0, tiled=True)  147 us
    all_gather x1, waiting for transfers between devices, on_device(): whole = lax.all_gather(moved, 'ep', axis=1, tiled=True)  55.2 us
    unnamed x11, local copies, waits for them, and re-layouts  17.8 us
    ppermute x1, waiting for transfers between devices, from_behind(): return lax.ppermute(x, axis, [(i, (i + by) % count) for i in range(count)])  14.5 us
    all_gather x1, local copies, waits for them, and re-layouts, on_device(): lax.all_gather(down_weight, 'fsdp', axis=0, tiled=True)  9.89 us
    all_to_all x1, waiting for transfers between devices, on_device(): lax.all_to_all(partial_latent, 'ep', split_axis=0, concat_axis=1, tiled=T...  8.77 us
    dot_general x1, matrix products, on_device(): jnp.dot(normed, lax.all_gather(down_weight, 'fsdp', axis=0, tiled=True),...  8.22 us
  transfers between devices with their start and end apart: 4, of which 4 were waited for; matrix products, arithmetic and copies ran while one was open for 1% of the time, Pallas kernels for 0%

commit v1 on v0

--- a/solution.py
+++ b/solution.py
@@ -35,7 +35,9 @@
 def on_device(hidden, attn_gain, q_gain, kv_gain, down_weight):
     row_count = hidden.shape[0]
     moved = from_behind(hidden, "section", 1)
-    whole = lax.all_gather(moved, "ep", axis=1, tiled=True)
+    whole = jnp.concatenate(
+        lax.all_to_all(jnp.stack([moved] * lax.axis_size("ep")), "ep", 0, 0), axis=1
+    )
     normed = root_scale(whole.astype(jnp.float32), attn_gain).astype(jnp.bfloat16)
     partial_latent = jnp.dot(
         normed,

time: 289 us -> 221 us (0.76)
  the two profiles are of different devices: /device:TPU:16 before, /device:TPU:8 now
where the time goes in v1:
time: 221 us; the launch traced here: 220 us
  waiting for transfers between devices  91.4 us (41%)
  local copies, waits for them, and re-layouts  47 us (21%)
  blocking collectives  46 us (21%)
  between operations  14.1 us (6%)
  matrix products  9.17 us (4%)
  starting transfers between devices  7.03 us (3%)
  other arithmetic  5.53 us (3%)
    all_gather x1, waiting for transfers between devices, on_device(): lax.all_gather(down_weight, 'fsdp', axis=0, tiled=True)  67.4 us
    all_to_all x1, blocking collectives, on_device(): lax.all_to_all(jnp.stack([moved] * lax.axis_size('ep')), 'ep', 0, 0)  46 us
    unnamed x11, local copies, waits for them, and re-layouts  18.6 us
    convert_element_type x2, local copies, waits for them, and re-layouts, on_device(): whole.astype(jnp.float32)  17.2 us
    ppermute x1, waiting for transfers between devices, from_behind(): return lax.ppermute(x, axis, [(i, (i + by) % count) for i in range(count)])  14.5 us
    all_gather x1, local copies, waits for them, and re-layouts, on_device(): lax.all_gather(down_weight, 'fsdp', axis=0, tiled=True)  9.89 us
    dot_general x1, matrix products, on_device(): jnp.dot(normed, lax.all_gather(down_weight, 'fsdp', axis=0, tiled=True),...  9.17 us
    all_to_all x1, waiting for transfers between devices, on_device(): lax.all_to_all(partial_latent, 'ep', split_axis=0, concat_axis=1, tiled=T...  8.77 us
  transfers between devices with their start and end apart: 3, of which 3 were waited for; matrix products, arithmetic and copies ran while one was open for 10% of the time, Pallas kernels for 0%

profile of v1, /device:TPU:8, one launch (start us, length us, event | category | flops | bytes accessed | tf_op | source)
XLA Modules:
  0.0 220.2 jit_solution(6659669099924211797)
XLA Ops:
  7.2 0.0 all-gather.3.cloned.1.call-start
  7.2 0.7 all-gather.3.cloned.1.call-update
  7.9 1.9 collective-permute-start
  9.8 14.5 %collective-permute-done = bf16[256,1792]{1,0:T(8,128)(2,1)S(1)} collective-permute-done((bf16[256,1792]{1,0:T(8,128)(2,1)}, bf16[256,1792]{1,0:T(8,128)(2,1)S(1)}, u32[]{:S(2)}, u32[]{:S(2)}) %collective-permute-start) | collective-permute-done | bytes 917536 | tf_op jit(solution)/shard_map/ppermute | solution.py:16
  24.3 0.2 stack.2
  24.6 46.0 %all_to_all.21 = bf16[4,256,1792]{2,1,0:T(8,128)(2,1)S(1)} all-to-all(bf16[4,256,1792]{2,1,0:T(8,128)(2,1)S(1)} %stack.2), channel_id=1, replica_groups=mesh['section'=4,'fsdp'=32,'ep'=4] {'ep'}, dimensions={0} | all-to-all | bytes 7340032 | tf_op jit(solution)/shard_map/all_to_all | solution.py:39
  70.5 1.8 copy-done
  72.3 0.8 fusion
  73.2 0.1 rsqrt.28
  73.3 2.7 %convert_bitcast_fusion = f32[256,4,1792]{2,0,1:T(8,128)S(1)} fusion(bf16[4,256,1792]{2,1,0:T(8,128)(2,1)} %copy-done), kind=kLoop, calls=%fused_computation.1 | loop fusion | flops 1835008 | bytes 11010048 | tf_op jit(solution)/shard_map/convert_element_type | solution.py:41
  76.0 7.7 %copy.15 = f32[256,4,1792]{2,1,0:T(4,128)} copy(f32[256,4,1792]{2,0,1:T(8,128)S(1)} %convert_bitcast_fusion) | data formatting | bytes 14680064 | tf_op jit(solution)/shard_map/convert_element_type | solution.py:41
  83.7 9.5 %reshape.81 = f32[4,64,7168]{2,1,0:T(8,128)} reshape(f32[256,4,1792]{2,1,0:T(4,128)} %copy.15) | data formatting | bytes 14680064 | tf_op jit(solution)/shard_map/convert_element_type | solution.py:41
  93.2 67.4 %all-gather.3.cloned.1.call-done = bf16[32,224,528]{1,2,0:T(8,128)(2,1)} async-done(((bf16[1,224,528]{1,2,0:T(8,128)(2,1)}), bf16[32,224,528]{1,2,0:T(8,128)(2,1)}) %all-gather.3.cloned.1.call-update) | async-done | bytes 7569424 | tf_op jit(solution)/shard_map/all_gather | solution.py:44
  160.6 9.9 %copy.16 = bf16[32,224,528]{1,0,2:T(8,128)(2,1)} copy(bf16[32,224,528]{1,2,0:T(8,128)(2,1)} %all-gather.3.cloned.1.call-done) | data formatting | bytes 15138816 | tf_op jit(solution)/shard_map/all_gather | solution.py:44
  170.5 16.6 %reshape.84 = bf16[7168,528,1]{0,1,2:T(8,128)(2,1)} reshape(bf16[32,224,528]{1,0,2:T(8,128)(2,1)} %copy.16) | data formatting | bytes 15138816
  187.1 0.0 copy-done.3
  187.1 9.2 %fusion.1 = f32[4,64,528]{2,1,0:T(8,128)} fusion(bf16[7168,528,1]{0,1,2:T(8,128)(2,1)} %reshape.84, f32[4,64,7168]{2,1,0:T(8,128)} %reshape.81, f32[7168]{0:T(1024)S(1)} %copy-done.3, f32[4,64]{1,0:T(4,128)S(1)} %rsqrt.28), kind=kOutput, calls=%fused_computation.4 | convolution fusion | flops 1943273472 | bytes 15479808 | tf_op jit(solution)/shard_map/dot_general | solution.py:42
  196.3 5.1 %all-to-all-start.1 = ((f32[4,64,528]{2,1,0:T(8,128)}), f32[4,64,528]{2,1,0:T(8,128)S(1)}, u32[]{:S(2)}, u32[]{:S(2)}) async-start(f32[4,64,528]{2,1,0:T(8,128)} %fusion.1), calls=%async_computation.1 | async-start | bytes 1310720 | tf_op jit(solution)/shard_map/all_to_all | solution.py:47
  201.4 8.8 %all-to-all-done.1 = f32[4,64,528]{2,1,0:T(8,128)S(1)} async-done(((f32[4,64,528]{2,1,0:T(8,128)}), f32[4,64,528]{2,1,0:T(8,128)S(1)}, u32[]{:S(2)}, u32[]{:S(2)}) %all-to-all-start.1) | async-done | bytes 540704 | tf_op jit(solution)/shard_map/all_to_all | solution.py:47
  210.2 0.4 copy.17
  210.6 0.3 all_to_all.18
  210.9 0.1 multiply_reduce_fusion.1
  211.0 0.1 multiply_reduce_fusion
  211.2 0.1 fusion.14
  211.3 0.1 copy.23
  211.3 0.1 copy.22
  211.4 0.2 fusion.9
  211.6 0.1 copy.20
  211.7 0.1 copy.21
  211.8 0.1 multiply_convert_fusion.3
  211.9 0.8 multiply_convert_fusion.2
  212.7 0.7 pad_maximum_fusion
  (11 shorter events, 0.0 us)
Async XLA Ops:
  7.2 153.4 %all-gather.3.cloned.1.call-start = ((), (), s32[]{:S(2)}) async-start(), calls=%async_computation.2 | async-start | bytes 8921088 | tf_op jit(solution)/shard_map/all_gather | solution.py:44
  7.9 16.4 %collective-permute-start = (bf16[256,1792]{1,0:T(8,128)(2,1)}, bf16[256,1792]{1,0:T(8,128)(2,1)S(1)}, u32[]{:S(2)}, u32[]{:S(2)}) collective-permute-start(bf16[256,1792]{1,0:T(8,128)(2,1)} %param.5), channel_id=1, source_target_pairs={{0,128},{128,256},{256,384},{384,0},{1,129},{129,257},{257,385},{3... | collective-permute-start | bytes 2752520 | tf_op jit(solution)/shard_map/ppermute | solution.py:16
  70.5 1.8 copy-start
  170.5 16.6 %copy-start.3 = (f32[7168]{0:T(1024)S(1)}, f32[7168]{0:T(1024)}, u32[]{:S(2)}) copy-start(f32[7168]{0:T(1024)} %param.6) | copy-start | bytes 86020
  187.1 24.7 %copy-start.2 = (f32[512]{0:T(512)S(1)}, f32[512]{0:T(512)}, u32[]{:S(2)}) copy-start(f32[512]{0:T(512)} %param.8) | copy-start | bytes 6148
  187.1 24.8 %copy-start.1 = (f32[1536]{0:T(1024)S(1)}, f32[1536]{0:T(1024)}, u32[]{:S(2)}) copy-start(f32[1536]{0:T(1024)} %param.7) | copy-start | bytes 18436
  196.3 13.9 %all-to-all-start.1 = ((f32[4,64,528]{2,1,0:T(8,128)}), f32[4,64,528]{2,1,0:T(8,128)S(1)}, u32[]{:S(2)}, u32[]{:S(2)}) async-start(f32[4,64,528]{2,1,0:T(8,128)} %fusion.1), calls=%async_computation.1 | async-start | bytes 1310720 | tf_op jit(solution)/shard_map/all_to_all | solution.py:47
Sparse Core Ops, SparseCore 0:
  10.0 150.4 all-gather.2
